TPU v7x, 32 devices: a whole 2x2x4 slice. The times are simulated.
32 devices in a mesh: heads: 1, seq: 32 (over z, y, x, core).
Axes of the slice: x: 2, y: 2, z: 4, core: 2. Of those that a mesh axis runs over, the one named last changes fastest.
Arguments:
- queries: bfloat16 [65536, 2, 512], P('seq', 'heads'), may hold values from -6 to 6
- key_rows: bfloat16 [65536, 2, 512], P('seq', 'heads'), may hold values from -6 to 6
- value_rows: bfloat16 [65536, 2, 512], P('seq', 'heads'), may hold values from -6 to 6
- step_rates: bfloat16 [2, 65536], P('heads', 'seq'), may hold values from 0.25 to 4
- live_counts: int32 [32], replicated, may hold values from 256 to 2048, as said below
- group_scales: float32 [2], P('heads'), may hold values from 0.4 to 1.8
- w_first: float32 [2, 512, 512], P('heads', 'seq'), may hold values from -0.8838835 to 0.8838835
- w_third: float32 [2, 512, 512], P('heads', 'seq'), may hold values from -0.8838835 to 0.8838835
- w_second: float32 [2, 512, 512], P('heads', 'seq'), may hold values from -0.8838835 to 0.8838835
Outputs:
- fast_out: bfloat16 [65536, 2, 512], P('seq', 'heads')
Inputs may be any that keep to these rules, and one draw needn't show every extreme that they name: `live_counts`: live token count of each clip shard; every draw has one shard of 2048 live tokens.
All inputs are finite; a program needn't handle non-finite values.
Results may differ from a plain program's by a relative error of at most 0.012.
The roundings to bfloat16 on the way count: a program that leaves them out, or rounds other values in their place, can miss the bound.
Values may be sent and summed in bfloat16 or wider, within the bound.
A program may use at most 128 MiB of HBM per device.

v0:
```python
import jax
import jax.numpy as jnp
from jax import lax
from jax.sharding import PartitionSpec as P

EPS = 1e-06


def row_normalize(start_w, update):
    norm_old = jnp.sqrt(jnp.mean(start_w * start_w, axis=-1, keepdims=True) + EPS)
    norm_new = jnp.sqrt(jnp.mean(update * update, axis=-1, keepdims=True) + EPS)
    return update * (norm_old / norm_new)


def group_terms(k_part, v_part, eta_col, b_one, b_three, b_two):
    h_one = jnp.dot(k_part, b_one, preferred_element_type=jnp.float32)
    h_three = jnp.dot(k_part, b_three, preferred_element_type=jnp.float32)
    gate = jax.nn.silu(h_one)
    act = (gate * h_three).astype(jnp.bfloat16)
    err = (eta_col[:, None] * v_part.astype(jnp.float32)).astype(jnp.bfloat16)
    back = jnp.dot(err, b_two.T, preferred_element_type=jnp.float32)
    sig = jax.nn.sigmoid(h_one)
    d_one = (back * h_three * (sig * (1.0 + h_one * (1.0 - sig)))).astype(jnp.bfloat16)
    d_three = (back * gate).astype(jnp.bfloat16)
    p_one = jnp.dot(k_part.T, d_one, preferred_element_type=jnp.float32)
    p_three = jnp.dot(k_part.T, d_three, preferred_element_type=jnp.float32)
    p_two = jnp.dot(act.T, err, preferred_element_type=jnp.float32)
    return (p_one, p_three, p_two)


def shard_terms(k_rows, v_rows, eta_rows, halves):
    b_one, b_three, b_two = halves
    firsts, thirds, seconds = ([], [], [])
    for group in range(k_rows.shape[1]):
        p_one, p_three, p_two = group_terms(
            k_rows[:, group],
            v_rows[:, group],
            eta_rows[:, group],
            b_one[group],
            b_three[group],
            b_two[group],
        )
        firsts.append(p_one)
        thirds.append(p_three)
        seconds.append(p_two)
    return (jnp.stack(firsts), jnp.stack(thirds), jnp.stack(seconds))


def apply_rows(q_rows, live_mask, fresh):
    c_one, c_three, c_two = fresh
    live_b = live_mask.astype(jnp.bfloat16)[:, None]
    pieces = []
    for group in range(q_rows.shape[1]):
        q_part = q_rows[:, group]
        q_one = jnp.dot(q_part, c_one[group], preferred_element_type=jnp.float32)
        q_three = jnp.dot(q_part, c_three[group], preferred_element_type=jnp.float32)
        a_query = (jax.nn.silu(q_one) * q_three).astype(jnp.bfloat16)
        o_part = jnp.dot(a_query, c_two[group], preferred_element_type=jnp.float32).astype(
            jnp.bfloat16
        )
        pieces.append(o_part * live_b)
    return jnp.stack(pieces, axis=1)


def shards(
    queries, key_rows, value_rows, step_rates, live_counts, group_scales, w_first, w_third, w_second
):
    cap_rows, groups, feat_width = queries.shape
    seq_size = lax.axis_size("seq")
    root_total = jnp.sqrt(jnp.float32(cap_rows * seq_size))
    own_index = lax.axis_index("seq")
    own_count = live_counts[own_index]
    position = jnp.arange(cap_rows, dtype=jnp.int32)
    live_mask = position < own_count
    full_rows = (
        lax.all_gather(w_first, "seq", axis=1, tiled=True),
        lax.all_gather(w_third, "seq", axis=1, tiled=True),
        lax.all_gather(w_second, "seq", axis=1, tiled=True),
    )
    halves = tuple((weight.astype(jnp.bfloat16) for weight in full_rows))
    eta_rows = (
        step_rates.T.astype(jnp.float32) * live_mask.astype(jnp.float32)[:, None] / root_total
    )
    sums = shard_terms(key_rows, value_rows, eta_rows, halves)
    summed = lax.psum((sums[0], sums[1], sums[2]), "seq")
    fresh = tuple(
        (
            row_normalize(weight, weight + term).astype(jnp.bfloat16)
            for weight, term in zip(full_rows, summed)
        )
    )
    fast = apply_rows(queries, live_mask, fresh)
    wide = fast.astype(jnp.float32) * group_scales[None, :, None]
    partial_sq = jnp.sum(wide * wide, axis=(1, 2))
    total_sq = lax.psum(partial_sq, "heads")
    denom = groups * feat_width * lax.axis_size("heads")
    factor = lax.rsqrt(total_sq / denom + EPS)[:, None, None]
    return (wide * factor).astype(jnp.bfloat16)


def solution(mesh):
    in_specs = (
        P("seq", "heads", None),
        P("seq", "heads", None),
        P("seq", "heads", None),
        P("heads", "seq"),
        P(),
        P("heads"),
        P("heads", "seq", None),
        P("heads", "seq", None),
        P("heads", "seq", None),
    )
    out_specs = P("seq", "heads", None)
    return jax.shard_map(shards, mesh=mesh, in_specs=in_specs, out_specs=out_specs, check_vma=False)
```

profile of v0, /device:TPU:19, one launch (start us, length us, event | category | flops | bytes accessed | tf_op | source)
XLA Modules:
  0.0 417.4 jit_solution(1568500695244042173)
XLA Ops:
  6.5 1.5 copy.110
  8.1 0.0 all-gather.4.cloned.1.call-update
  8.1 0.0 all-gather.8.cloned.1.call-start
  8.1 1.5 copy.113
  9.7 0.0 all-gather.8.cloned.1.call-update
  9.7 0.0 all-gather.6.cloned.1.call-start
  9.7 0.7 all-gather.6.cloned.1.call-update
  10.4 0.0 all-reduce.3.cloned.1.call-start
  10.5 1.3 dynamic_slice.3
  11.8 0.7 fusion.62
  12.5 0.0 copy-start.17
  12.5 9.3 %fusion.74 = (bf16[2048,1,512]{2,1,0:T(2,128)(2,1)S(1)}, bf16[2048,1,512]{2,1,0:T(2,128)(2,1)S(1)}) fusion(bf16[2048,2,512]{2,1,0:T(2,128)(2,1)} %param.10), kind=kLoop, calls=%fused_computation.122 | loop fusion | bytes 8388608 | tf_op jit(solution)/shard_map/slice | solution.py:36
  21.8 0.0 copy-start.4
  21.8 2.6 copy_bitcast_fusion.2
  24.4 7.4 %fusion.73 = (bf16[2048,1,512]{2,1,0:T(2,128)(2,1)}, bf16[2048,1,512]{2,1,0:T(2,128)(2,1)}) fusion(bf16[2048,2,512]{2,1,0:T(2,128)(2,1)S(1)} %copy-done.4), kind=kLoop, calls=%fused_computation.121 | loop fusion | bytes 8388608 | tf_op jit(solution)/shard_map/slice | solution.py:37
  31.8 34.3 %all-gather.4.cloned.1.call-done = f32[2,512,512]{2,0,1:T(2,128)} async-done(((f32[2,16,512]{2,0,1:T(2,128)}), f32[2,512,512]{2,0,1:T(2,128)}) %all-gather.4.cloned.1.call-update) | async-done | bytes 2097168 | tf_op jit(solution)/shard_map/all_gather | solution.py:76
  66.1 1.9 copy.167
  68.0 56.0 %all-gather.8.cloned.1.call-done = f32[2,512,512]{2,0,1:T(2,128)} async-done(((f32[2,16,512]{2,0,1:T(2,128)}), f32[2,512,512]{2,0,1:T(2,128)}) %all-gather.8.cloned.1.call-update) | async-done | bytes 2097168 | tf_op jit(solution)/shard_map/all_gather | solution.py:77
  124.1 1.9 copy.168
  126.0 3.2 fusion.60
  129.2 3.2 fusion.61
  132.4 3.3 fusion.58
  135.7 3.2 fusion.59
  138.9 43.2 %all-gather.6.cloned.1.call-done = f32[2,512,512]{2,1,0:T(8,128)} async-done(((f32[2,16,512]{2,1,0:T(8,128)}), f32[2,512,512]{2,1,0:T(8,128)}) %all-gather.6.cloned.1.call-update) | async-done | bytes 2097168 | tf_op jit(solution)/shard_map/all_gather | solution.py:78
  182.1 1.9 convert_element_type.111
  184.0 3.6 fusion.26
  187.6 0.0 copy-done.12
  187.7 4.4 %fusion.40 = f32[1,512,512]{2,1,0:T(8,128)S(1)} fusion(f32[2048]{0:T(1024)S(1)} %bitcast.158, f32[2048,512]{1,0:T(8,128)S(1)} %copy-done.13, bf16[2048,1,512]{2,1,0:T(2,128)(2,1)} %get-tuple-element.17, f32[2048,512]{1,0:T(8,128)S(1)} %copy-done.12), kind=kOutput, calls=%fused_computation.78 | convolution fusion | flops 1083179008 | bytes 11542528 | tf_op jit(solution)/shard_map/dot_general | solution.py:27
  192.0 2.4 fusion.38
  194.5 1.3 fusion.46
  195.8 0.8 copy-done.14
  196.6 1.3 fusion.30
  198.0 1.4 copy-done.10
  199.3 2.1 fusion.43
  201.5 2.4 fusion.39
  203.9 1.3 fusion.47
  205.2 1.5 pad_maximum_fusion.1
  206.7 1.5 pad_maximum_fusion.3
  208.2 1.6 pad_maximum_fusion.2
  209.8 0.0 all-reduce.3.cloned.1.call-update
  209.8 10.1 %fusion.72 = (bf16[2048,1,512]{2,1,0:T(2,128)(2,1)}, bf16[2048,1,512]{2,1,0:T(2,128)(2,1)}) fusion(bf16[2048,2,512]{2,1,0:T(2,128)(2,1)} %param.9), kind=kLoop, calls=%fused_computation.120 | loop fusion | bytes 8388608 | tf_op jit(solution)/shard_map/slice | solution.py:54
  220.0 0.9 multiply_reduce_fusion.4
  220.9 0.1 copy.123
  221.0 0.9 multiply_reduce_fusion.6
  221.9 0.1 copy.119
  222.0 4.2 %copy.122 = f32[2,512,512]{1,2,0:T(8,128)} copy(f32[2,512,512]{2,0,1:T(2,128)} %all-gather.8.cloned.1.call-done) | data formatting | bytes 4194304 | tf_op jit(solution)/shard_map/all_gather | solution.py:77
  226.1 3.0 copy.118
  229.1 137.1 %all-reduce.3.cloned.1.call-done = (f32[2,512,512]{1,2,0:T(8,128)}, f32[2,512,512]{2,1,0:T(8,128)}, f32[2,512,512]{1,2,0:T(8,128)}) async-done(((f32[2,512,512]{1,2,0:T(8,128)}, f32[2,512,512]{2,1,0:T(8,128)}, f32[2,512,512]{1,2,0:T(8,128)}), (f32[2,512,512]{1,2,0:T(8,128)}, f32[2,512,512]{2,1,0:T(8,128)}, f32[2,512,512]{1,2,0:T(8,128)})) %all-reduce.3.cloned.1.call-update) | async-done | bytes 6291472 | tf_op jit(solution)/shard_map/psum | solution.py:85
  366.3 2.9 multiply_reduce_fusion.5
  369.2 0.3 multiply_convert_fusion.13
  369.5 0.2 copy-done.6
  369.7 3.3 fusion.48
  373.0 3.3 fusion.49
  376.3 0.5 multiply_reduce_fusion.3
  376.8 0.3 multiply_convert_fusion.12
  377.1 0.7 copy-done.8
  377.8 0.6 copy-done.15
  378.5 0.5 multiply_reduce_fusion.1
  379.0 1.2 multiply_convert_fusion.11
  380.2 6.2 %fusion.17 = bf16[2048,1,512]{0,2,1:T(8,128)(2,1)S(1)} fusion(bf16[2048]{0:T(1024)(128)(2,1)S(1)} %get-tuple-element.23, f32[512,2048]{0,1:T(8,128)} %fusion.48, bf16[2048,1,512]{2,1,0:T(2,128)(2,1)} %get-tuple-element.14, bf16[2,512,512]{2,1,0:T(8,128)(2,1)} %multiply_convert_fusion.11, bf16[2,512,512]{1,2,0:T(8,128)(2,1)S(1)} %multiply_convert_fusion.12), kind=kOutput, calls=%fused_computation.41 | convolution fusion | flops 2159017984 | bytes 11538432 | tf_op jit(solution)/shard_map/dot_general | solution.py:58
  386.4 7.6 %fusion.19 = bf16[2048,1,512]{0,2,1:T(8,128)(2,1)} fusion(bf16[2048]{0:T(1024)(128)(2,1)S(1)} %get-tuple-element.23, f32[512,2048]{0,1:T(8,128)} %fusion.49, bf16[2048,1,512]{2,1,0:T(2,128)(2,1)} %get-tuple-element.15, bf16[2,512,512]{2,1,0:T(8,128)(2,1)} %multiply_convert_fusion.11, bf16[2,512,512]{1,2,0:T(8,128)(2,1)S(1)} %multiply_convert_fusion.12), kind=kOutput, calls=%fused_computation.43 | convolution fusion | flops 2159017984 | bytes 11538432 | tf_op jit(solution)/shard_map/dot_general | solution.py:58
  394.0 2.8 multiply_reduce_fusion
  396.8 2.7 multiply_convert_fusion
  399.5 11.1 %copy.128 = bf16[2048,2,512]{2,1,0:T(2,128)(2,1)} copy(bf16[2048,2,512]{0,2,1:T(8,128)(2,1)} %multiply_convert_fusion) | data formatting | bytes 8388608 | tf_op jit(solution)/shard_map/convert_element_type | solution.py:98
  (37 shorter events, 0.2 us)
Async XLA Ops:
  6.5 59.6 %all-gather.4.cloned.1.call-start = ((), (), s32[]{:S(2)}) async-start(), calls=%async_computation | async-start | bytes 2162688 | tf_op jit(solution)/shard_map/all_gather | solution.py:76
  8.1 116.0 %all-gather.8.cloned.1.call-start = ((), (), s32[]{:S(2)}) async-start(), calls=%async_computation.2 | async-start | bytes 2162688 | tf_op jit(solution)/shard_map/all_gather | solution.py:77
  9.7 172.4 %all-gather.6.cloned.1.call-start = ((), (), s32[]{:S(2)}) async-start(), calls=%async_computation.1 | async-start | bytes 2162688 | tf_op jit(solution)/shard_map/all_gather | solution.py:78
  10.4 355.8 %all-reduce.3.cloned.1.call-start = ((), (), s32[]{:S(2)}) async-start(), calls=%async_computation.3 | async-start | bytes 12582912 | tf_op jit(solution)/shard_map/psum | solution.py:85
  12.5 9.3 %copy-start.17 = (bf16[2,2048]{1,0:T(2,128)(2,1)S(1)}, bf16[2,2048]{1,0:T(2,128)(2,1)}, u32[]{:S(2)}) copy-start(bf16[2,2048]{1,0:T(2,128)(2,1)} %param.12) | copy-start | bytes 24580
  21.8 2.6 copy-start.4
  129.2 3.2 copy-start
  182.1 5.5 %copy-start.13 = (f32[2048,512]{1,0:T(8,128)S(1)}, f32[2048,512]{1,0:T(8,128)}, u32[]{:S(2)}) copy-start(f32[2048,512]{1,0:T(8,128)} %fusion.59) | copy-start | bytes 12582916
  184.0 3.7 copy-start.12
  187.7 4.4 %copy-start.1 = (bf16[2048,512]{1,0:T(8,128)(2,1)S(1)}, bf16[2048,512]{1,0:T(8,128)(2,1)}, u32[]{:S(2)}) copy-start(bf16[2048,512]{1,0:T(8,128)(2,1)} %get-tuple-element.25) | copy-start | bytes 6291460
  194.4 2.2 copy-start.14
  194.5 3.5 copy-start.11
  195.8 3.5 copy-start.10
  209.8 10.1 %copy-start.3 = (f32[2,512,512]{2,0,1:T(2,128)S(1)}, f32[2,512,512]{2,0,1:T(2,128)}, u32[]{:S(2)}) copy-start(f32[2,512,512]{2,0,1:T(2,128)} %all-gather.8.cloned.1.call-done) | copy-start | bytes 6291460
  209.8 11.1 %copy-start.2 = (f32[2,512,512]{2,0,1:T(2,128)S(1)}, f32[2,512,512]{2,0,1:T(2,128)}, u32[]{:S(2)}) copy-start(f32[2,512,512]{2,0,1:T(2,128)} %all-gather.4.cloned.1.call-done) | copy-start | bytes 6291460
  366.3 3.4 copy-start.6
  369.5 3.5 copy-start.5
  373.0 3.3 copy-start.9
  373.0 3.3 copy-start.16
  376.3 1.6 copy-start.8
  376.3 2.2 copy-start.15
  386.4 7.6 %copy-start.18 = (f32[2]{0:T(128)S(1)}, f32[2]{0:T(128)}, u32[]{:S(2)}) copy-start(f32[2]{0:T(128)} %param.14) | copy-start | bytes 28
  394.0 2.8 copy-start.7
Sparse Core Ops, SparseCore 0:
  10.2 55.8 all-gather.3
  69.0 55.0 all-gather.7
  127.0 55.0 all-gather.5
  209.9 156.2 all-reduce.2
where the time goes:
time: 424 us; the launch traced here: 417 us
  waiting for transfers between devices  271 us (64%)
  local copies, waits for them, and re-layouts  59.9 us (14%)
  matrix products  52.2 us (12%)
  other arithmetic  20.3 us (5%)
  between operations  13.6 us (3%)
    psum x1, waiting for transfers between devices, shards(): summed = lax.psum((sums[0], sums[1], sums[2]), 'seq')  137 us
    all_gather x1, waiting for transfers between devices, shards(): lax.all_gather(w_third, 'seq', axis=1, tiled=True)  56 us
    all_gather x1, waiting for transfers between devices, shards(): lax.all_gather(w_second, 'seq', axis=1, tiled=True)  43.2 us
    all_gather x1, waiting for transfers between devices, shards(): lax.all_gather(w_first, 'seq', axis=1, tiled=True)  34.3 us
    dot_general x2, matrix products, apply_rows(): jnp.dot(a_query, c_two[group], preferred_element_type=jnp.float32)  13.8 us
    convert_element_type x1, local copies, waits for them, and re-layouts, shards(): return (wide * factor).astype(jnp.bfloat16)  11.1 us
    slice x1, local copies, waits for them, and re-layouts, apply_rows(): q_part = q_rows[:, group]  10.1 us
    slice x1, local copies, waits for them, and re-layouts, shard_terms(): k_rows[:, group]  9.27 us
  transfers between devices with their start and end apart: 4, of which 4 were waited for; matrix products, arithmetic and copies ran while one was open for 14% of the time, Pallas kernels for 0%

commit v1 on v0

v1 whole, which is shorter than its diff:
```python
import functools

import jax
import jax.numpy as jnp
from jax import lax
from jax.experimental import pallas as pl
from jax.experimental.pallas import tpu as pltpu
from jax.sharding import PartitionSpec as P

EPS = 1e-06
MESH = pl.DeviceIdType.MESH
LANES = 128
VMEM_LIMIT = 60 * 1024 * 1024


def ring_maps(chips):
    if chips != 16:
        return (lambda chip: chip), (lambda pos: pos)

    def pos_of(chip):
        z, y, x = chip // 4, (chip // 2) % 2, chip % 2
        p = y * 3 + x - 2 * x * y
        row = 3 - z
        odd = row % 2
        m = (1 - odd) * (p - 1) + odd * (3 - p)
        snake = 4 + 3 * row + m
        off = (p + 3) // 4
        return (1 - off) * z + off * snake

    def chip_of(pos):
        on = pos // 4
        on = (on + 3) // 4
        k = (pos + 12) % 16
        row = k // 3
        m = k % 3
        odd = row % 2
        p = (1 - odd) * (m + 1) + odd * (3 - m)
        z = (1 - on) * pos + on * (3 - row)
        p = on * p
        y = p // 2
        x = (y + p) % 2
        return z * 4 + y * 2 + x

    return pos_of, chip_of


class Ring:
    def __init__(self, n):
        self.chips = n // 2
        self.pos_of, self.chip_of = ring_maps(self.chips)
        me = lax.axis_index("seq")
        self.core = me % 2
        self.partner = me + 1 - 2 * self.core
        self.chip = me // 2
        self.pos = self.pos_of(self.chip)
        self.right_steps = self.chips // 2
        self.left_steps = self.chips - 1 - self.right_steps
        self.right = self.index(1)
        self.left = self.index(-1)

    def index(self, offset):
        return self.chip_at(offset) * 2 + self.core

    def chip_at(self, offset):
        return self.chip_of((self.pos + offset + self.chips) % self.chips)

    def barrier(self):
        sem = pltpu.get_barrier_semaphore()
        for peer in (self.left, self.right, self.partner):
            pl.semaphore_signal(sem, inc=1, device_id={"seq": peer}, device_id_type=MESH)
        pl.semaphore_wait(sem, 3)


def remote(src, dst, send_sem, recv_sem, peer):
    return pltpu.make_async_remote_copy(
        src_ref=src, dst_ref=dst, send_sem=send_sem, recv_sem=recv_sem,
        device_id={"seq": peer}, device_id_type=MESH,
    )


def gather_ring(ring, own, out, sems):
    groups = own.shape[0]
    rs, rr, ls, lr, ps, pr = sems
    me = lax.axis_index("seq")
    for g in range(groups):
        out[g, :, me] = own[g]

    def slot(g, idx):
        return out.at[g, :, idx]

    def right_copy(s, g, src):
        dst = slot(g, ring.index(-s))
        return remote(dst if src is None else src, dst, rs.at[s, g], rr.at[s, g], ring.right)

    def left_copy(s, g, src):
        dst = slot(g, ring.index(s))
        return remote(dst if src is None else src, dst, ls.at[s, g], lr.at[s, g], ring.left)

    def partner_copy(k, g, offset, src):
        dst = slot(g, ring.index(offset))
        return remote(dst if src is None else src, dst, ps.at[k, g], pr.at[k, g], ring.partner)

    for g in range(groups):
        right_copy(0, g, own.at[g]).start()
        left_copy(0, g, own.at[g]).start()
        partner_copy(0, g, 0, own.at[g]).start()

    def step(s, carry):
        for g in range(groups):
            right_copy(s - 1, g, None).wait_recv()

            @pl.when(s < ring.right_steps)
            def _():
                right_copy(s, g, None).start()

            partner_copy(s, g, -s, None).start()

            @pl.when(s <= ring.left_steps)
            def _():
                left_copy(s - 1, g, None).wait_recv()

                @pl.when(s < ring.left_steps)
                def _():
                    left_copy(s, g, None).start()

                partner_copy(ring.right_steps + s, g, s, None).start()

        return carry

    lax.fori_loop(1, ring.right_steps + 1, step, 0)

    def drain(s, carry):
        for g in range(groups):
            right_copy(s, g, None).wait_send()

            @pl.when(s < ring.left_steps)
            def _():
                left_copy(s, g, None).wait_send()

        return carry

    lax.fori_loop(0, ring.right_steps, drain, 0)

    def drain_partner(k, carry):
        for g in range(groups):
            copy = partner_copy(k, g, 0, None)
            copy.wait_send()
            copy.wait_recv()
        return carry

    lax.fori_loop(0, ring.chips, drain_partner, 0)


def gather_sems(ring_chips, groups):
    right = ring_chips // 2
    left = max(ring_chips - 1 - right, 1)
    dma = pltpu.SemaphoreType.DMA
    return [dma((right, groups)), dma((right, groups)), dma((left, groups)), dma((left, groups)),
            dma((ring_chips, groups)), dma((ring_chips, groups))]


def gather_kernel(n, own_ref, out_ref, *sems):
    ring = Ring(n)
    ring.barrier()
    gather_ring(ring, own_ref, out_ref, sems)


def gather_rows(n, own):
    groups, kinds, rows, feats = own.shape
    return pl.pallas_call(
        functools.partial(gather_kernel, n),
        out_shape=jax.ShapeDtypeStruct((groups, kinds, n, rows, feats), own.dtype),
        in_specs=[pl.BlockSpec(memory_space=pltpu.VMEM)],
        out_specs=pl.BlockSpec(memory_space=pltpu.VMEM),
        scratch_shapes=gather_sems(n // 2, groups),
        compiler_params=pltpu.CompilerParams(
            collective_id=0, has_side_effects=True, vmem_limit_bytes=VMEM_LIMIT
        ),
        name="gather_start",
    )(own)


def reduce_kernel(n, part_ref, w_ref, out_ref, pair, pair_in, buf_r, buf_l, in_r, in_l, fresh,
                  xs, xr, rs, rr, ls, lr, *gsems):
    ring = Ring(n)
    groups = w_ref.shape[0]
    ring.barrier()
    exchange = [
        remote(part_ref.at[g, :, :, 1 - ring.core], pair_in.at[g], xs.at[g], xr.at[g], ring.partner)
        for g in range(groups)
    ]
    for copy in exchange:
        copy.start()

    def right_copy(s, g):
        return remote(buf_r.at[s, g], in_r.at[s, g], rs.at[s, g], rr.at[s, g], ring.right)

    def left_copy(s, g):
        return remote(buf_l.at[s, g], in_l.at[s, g], ls.at[s, g], lr.at[s, g], ring.left)

    def both(g, chip):
        return (part_ref[g, :, chip, ring.core].astype(jnp.float32)
                + pair_in[g, :, chip].astype(jnp.float32))

    for g in range(groups):
        exchange[g].wait_recv()
        buf_r[0, g] = both(g, ring.chip_at(ring.right_steps)).astype(buf_r.dtype)
        right_copy(0, g).start()
        buf_l[0, g] = both(g, ring.chip_at(-ring.left_steps)).astype(buf_l.dtype)
        left_copy(0, g).start()

    def step(s, carry):
        for g in range(groups):
            own = both(g, ring.chip_at(ring.right_steps - s))
            right_copy(s - 1, g).wait_recv()
            buf_r[s, g] = (own + in_r[s - 1, g].astype(jnp.float32)).astype(buf_r.dtype)
            right_copy(s, g).start()

            @pl.when(s < ring.left_steps)
            def _():
                own_l = both(g, ring.chip_at(s - ring.left_steps))
                left_copy(s - 1, g).wait_recv()
                buf_l[s, g] = (own_l + in_l[s - 1, g].astype(jnp.float32)).astype(buf_l.dtype)
                left_copy(s, g).start()

        return carry

    lax.fori_loop(1, ring.right_steps, step, 0)
    for g in range(groups):
        left_copy(ring.left_steps - 1, g).wait_recv()
        right_copy(ring.right_steps - 1, g).wait_recv()
        term = (both(g, ring.chip) + in_l[ring.left_steps - 1, g].astype(jnp.float32)
                + in_r[ring.right_steps - 1, g].astype(jnp.float32))
        start_w = w_ref[g]
        update = start_w + term
        norm_old = jnp.sqrt(jnp.mean(start_w * start_w, axis=-1, keepdims=True) + EPS)
        norm_new = jnp.sqrt(jnp.mean(update * update, axis=-1, keepdims=True) + EPS)
        fresh[g] = (update * (norm_old / norm_new)).astype(fresh.dtype)

    gather_ring(ring, fresh, out_ref, gsems)
    for g in range(groups):
        exchange[g].wait_send()

    def drain(s, carry):
        for g in range(groups):
            right_copy(s, g).wait_send()

            @pl.when(s < ring.left_steps)
            def _():
                left_copy(s, g).wait_send()

        return carry

    lax.fori_loop(0, ring.right_steps, drain, 0)


def reduce_rows(n, part, w_own):
    groups, kinds, rows, feats = w_own.shape
    chips = n // 2
    right = chips // 2
    left = chips - 1 - right
    piece = (groups, kinds, rows, feats)
    dma = pltpu.SemaphoreType.DMA
    bf = jnp.bfloat16
    return pl.pallas_call(
        functools.partial(reduce_kernel, n),
        out_shape=jax.ShapeDtypeStruct((groups, kinds, n, rows, feats), bf),
        in_specs=[pl.BlockSpec(memory_space=pltpu.VMEM)] * 2,
        out_specs=pl.BlockSpec(memory_space=pltpu.VMEM),
        scratch_shapes=[
            pltpu.VMEM((8, LANES), bf),
            pltpu.VMEM((groups, kinds, chips, rows, feats), bf),
            pltpu.VMEM((right,) + piece, bf),
            pltpu.VMEM((left,) + piece, bf),
            pltpu.VMEM((right,) + piece, bf),
            pltpu.VMEM((left,) + piece, bf),
            pltpu.VMEM(piece, bf),
            dma((groups,)), dma((groups,)),
            dma((right, groups)), dma((right, groups)),
            dma((left, groups)), dma((left, groups)),
        ] + gather_sems(chips, groups),
        compiler_params=pltpu.CompilerParams(
            collective_id=1, has_side_effects=True, vmem_limit_bytes=VMEM_LIMIT
        ),
        name="reduce_gather",
    )(part, w_own)


def to_view(rows):
    tokens, groups, feats = rows.shape
    cuts = feats // LANES
    return rows.reshape(tokens, groups, cuts, LANES).transpose(0, 2, 1, 3).reshape(-1, LANES)


def from_view(view, shape):
    tokens, groups, feats = shape
    cuts = feats // LANES
    return view.reshape(tokens, cuts, groups, LANES).transpose(0, 2, 1, 3).reshape(shape)


def pick(scr, g, groups, cuts, tile):
    step = groups * cuts
    cols = [scr[pl.ds(c * groups + g, tile, stride=step), :] for c in range(cuts)]
    return jnp.concatenate(cols, axis=-1).astype(jnp.bfloat16)


def dot(a, b, dims):
    return lax.dot_general(a, b, (dims, ((), ())), preferred_element_type=jnp.float32)


def sigmoid(x):
    return 0.5 * jnp.tanh(0.5 * x) + 0.5


def terms_kernel(groups, cuts, tile, k_ref, v_ref, eta_ref, b_ref, out_ref, k_scr, v_scr, acc):
    i = pl.program_id(0)

    @pl.when(i == 0)
    def _():
        acc[...] = jnp.zeros_like(acc)

    k_scr[...] = k_ref[...].astype(jnp.float32)
    v_scr[...] = v_ref[...].astype(jnp.float32)
    for g in range(groups):
        k = pick(k_scr, g, groups, cuts, tile)
        v = pick(v_scr, g, groups, cuts, tile)
        err = (eta_ref[:, g:g + 1] * v.astype(jnp.float32)).astype(jnp.bfloat16)
        h_one = dot(k, b_ref[g, 0], ((1,), (0,)))
        h_three = dot(k, b_ref[g, 1], ((1,), (0,)))
        back = dot(err, b_ref[g, 2], ((1,), (1,)))
        sig = sigmoid(h_one)
        gate = h_one * sig
        act = (gate * h_three).astype(jnp.bfloat16)
        d_one = (back * h_three * (sig * (1.0 + h_one * (1.0 - sig)))).astype(jnp.bfloat16)
        d_three = (back * gate).astype(jnp.bfloat16)
        acc[g, 0] += dot(k, d_one, ((0,), (0,)))
        acc[g, 1] += dot(k, d_three, ((0,), (0,)))
        acc[g, 2] += dot(act, err, ((0,), (0,)))

    @pl.when(i == pl.num_programs(0) - 1)
    def _():
        out_ref[...] = acc[...].astype(out_ref.dtype)


def local_terms(k_view, v_view, eta_rows, halves):
    groups, kinds, width, feats = halves.shape
    cuts = feats // LANES
    tokens = eta_rows.shape[0]
    tile = min(512, tokens)
    rows = tile * groups * cuts
    whole = pl.BlockSpec(memory_space=pltpu.VMEM)
    return pl.pallas_call(
        functools.partial(terms_kernel, groups, cuts, tile),
        grid=(tokens // tile,),
        out_shape=jax.ShapeDtypeStruct(halves.shape, jnp.bfloat16),
        in_specs=[
            pl.BlockSpec((rows, LANES), lambda i: (i, 0)),
            pl.BlockSpec((rows, LANES), lambda i: (i, 0)),
            pl.BlockSpec((tile, groups), lambda i: (i, 0)),
            whole,
        ],
        out_specs=whole,
        scratch_shapes=[
            pltpu.VMEM((rows, LANES), jnp.float32),
            pltpu.VMEM((rows, LANES), jnp.float32),
            pltpu.VMEM(halves.shape, jnp.float32),
        ],
        compiler_params=pltpu.CompilerParams(vmem_limit_bytes=VMEM_LIMIT),
        name="local_terms",
    )(k_view, v_view, eta_rows, halves)


def apply_kernel(groups, cuts, tile, denom, count_ref, scale_ref, q_ref, c_ref, out_ref, q_scr, o_scr):
    i = pl.program_id(0)
    step = groups * cuts
    position = i * tile + lax.broadcasted_iota(jnp.int32, (tile, 1), 0)
    live = (position < count_ref[0]).astype(jnp.float32)
    q_scr[...] = q_ref[...].astype(jnp.float32)
    pieces = []
    total_sq = jnp.zeros((tile, 1), jnp.float32)
    for g in range(groups):
        q = pick(q_scr, g, groups, cuts, tile)
        q_one = dot(q, c_ref[g, 0], ((1,), (0,)))
        q_three = dot(q, c_ref[g, 1], ((1,), (0,)))
        a_query = (q_one * sigmoid(q_one) * q_three).astype(jnp.bfloat16)
        o = dot(a_query, c_ref[g, 2], ((1,), (0,))).astype(jnp.bfloat16)
        o = o.astype(jnp.float32) * live
        if denom is not None:
            o = o * scale_ref[g]
            total_sq = total_sq + jnp.sum(o * o, axis=-1, keepdims=True)
        pieces.append(o)
    if denom is not None:
        factor = lax.rsqrt(total_sq / denom + EPS)
        pieces = [o * factor for o in pieces]
    for g in range(groups):
        for c in range(cuts):
            o_scr[pl.ds(c * groups + g, tile, stride=step), :] = pieces[g][:, c * LANES:(c + 1) * LANES]
    out_ref[...] = o_scr[...].astype(out_ref.dtype)


def apply_rows(q_view, count, scales, fresh, tokens, denom):
    groups, kinds, width, feats = fresh.shape
    cuts = feats // LANES
    tile = min(512, tokens)
    rows = tile * groups * cuts
    smem = pl.BlockSpec(memory_space=pltpu.SMEM)
    return pl.pallas_call(
        functools.partial(apply_kernel, groups, cuts, tile, denom),
        grid=(tokens // tile,),
        out_shape=jax.ShapeDtypeStruct(q_view.shape, jnp.bfloat16),
        in_specs=[
            smem,
            smem,
            pl.BlockSpec((rows, LANES), lambda i: (i, 0)),
            pl.BlockSpec(memory_space=pltpu.VMEM),
        ],
        out_specs=pl.BlockSpec((rows, LANES), lambda i: (i, 0)),
        scratch_shapes=[
            pltpu.VMEM((rows, LANES), jnp.float32),
            pltpu.VMEM((rows, LANES), jnp.float32),
        ],
        compiler_params=pltpu.CompilerParams(vmem_limit_bytes=VMEM_LIMIT),
        name="apply_rows",
    )(count, scales, q_view, fresh)


def shards(
    queries, key_rows, value_rows, step_rates, live_counts, group_scales, w_first, w_third, w_second
):
    cap_rows, groups, feat_width = queries.shape
    seq_size = lax.axis_size("seq")
    heads = lax.axis_size("heads")
    root_total = jnp.sqrt(jnp.float32(cap_rows * seq_size))
    own_count = lax.dynamic_slice(live_counts, (lax.axis_index("seq"),), (1,))
    live_mask = jnp.arange(cap_rows, dtype=jnp.int32) < own_count[0]
    eta_rows = (
        step_rates.T.astype(jnp.float32) * live_mask.astype(jnp.float32)[:, None] / root_total
    )
    w_own = jnp.stack([w_first, w_third, w_second], axis=1)
    full = (groups, 3, feat_width, feat_width)
    chips = seq_size // 2
    own_rows = w_own.shape[2]
    halves = gather_rows(seq_size, w_own.astype(jnp.bfloat16)).reshape(full)
    part = local_terms(to_view(key_rows), to_view(value_rows), eta_rows, halves)
    part = part.reshape(groups, 3, chips, 2, own_rows, feat_width)
    fresh = reduce_rows(seq_size, part, w_own).reshape(full)
    denom = groups * feat_width * heads
    view = apply_rows(
        to_view(queries), own_count, group_scales, fresh, cap_rows, denom if heads == 1 else None
    )
    fast = from_view(view, queries.shape)
    if heads == 1:
        return fast
    wide = fast.astype(jnp.float32) * group_scales[None, :, None]
    total_sq = lax.psum(jnp.sum(wide * wide, axis=(1, 2)), "heads")
    factor = lax.rsqrt(total_sq / denom + EPS)[:, None, None]
    return (wide * factor).astype(jnp.bfloat16)


def solution(mesh):
    in_specs = (
        P("seq", "heads", None),
        P("seq", "heads", None),
        P("seq", "heads", None),
        P("heads", "seq"),
        P(),
        P("heads"),
        P("heads", "seq", None),
        P("heads", "seq", None),
        P("heads", "seq", None),
    )
    out_specs = P("seq", "heads", None)
    return jax.shard_map(shards, mesh=mesh, in_specs=in_specs, out_specs=out_specs, check_vma=False)
```

time: 424 us -> 144 us (0.34)
  waiting for transfers between devices: 271 us -> 0 us
  Pallas kernels: 0 us -> 135 us
  local copies, waits for them, and re-layouts: 59.9 us -> 2.6 us
  matrix products: 52.2 us -> 0 us
  other arithmetic: 20.3 us -> 3.53 us
  between operations: 13.6 us -> 0.06 us
    psum x1 -> x0, waiting for transfers between devices: 137 us -> none  [shards(): summed = lax.psum((sums[0], sums[1], sums[2]), 'seq')]
    pallas_call x0 -> x4, Pallas kernels: none -> 135 us  [the longest x1 65 us: reduce_rows(): pl.pallas_call(functools.partial(reduce_kernel, n), out_shape=jax.ShapeDt...]
    all_gather x3 -> x0, waiting for transfers between devices: 134 us -> none  [the longest x1 56 us: shards(): lax.all_gather(w_third, 'seq', axis=1, tiled=True)]
    dot_general x16 -> x0, matrix products: 52.2 us -> none  [the longest x2 13.8 us: apply_rows(): jnp.dot(a_query, c_two[group], preferred_element_type=jnp.float32)]
    slice x4 -> x0, local copies, waits for them, and re-layouts: 26.8 us -> none  [the longest x1 10.1 us: apply_rows(): q_part = q_rows[:, group]]
    convert_element_type x1 -> x0, local copies, waits for them, and re-layouts: 11.1 us -> none  [shards(): return (wide * factor).astype(jnp.bfloat16)]
    all_gather x4 -> x0, local copies, waits for them, and re-layouts: 11 us -> none  [the longest x2 6.07 us: shards(): lax.all_gather(w_third, 'seq', axis=1, tiled=True)]
    reduce_sum x6 -> x0, other arithmetic: 8.48 us -> none  [the longest x3 3.9 us: row_normalize(): norm_new = jnp.sqrt(jnp.mean(update * update, axis=-1, keepdims=True) + EPS)]
  transfers between devices with their start and end apart: 4 -> 0, of which waited for: 4 -> 0; matrix products, arithmetic and copies ran while one was open for 14% -> 0% of each run, Pallas kernels for 0% -> 0%
where the time goes in v1:
time: 144 us; the launch traced here: 141 us
  Pallas kernels  135 us (94%)
  other arithmetic  3.53 us (2%)
  local copies, waits for them, and re-layouts  2.6 us (2%)
    pallas_call x1, Pallas kernels, reduce_rows(): pl.pallas_call(functools.partial(reduce_kernel, n), out_shape=jax.ShapeDt...  65 us
    pallas_call x1, Pallas kernels, gather_rows(): pl.pallas_call(functools.partial(gather_kernel, n), out_shape=jax.ShapeDt...  33.4 us
    pallas_call x1, Pallas kernels, local_terms(): pl.pallas_call(functools.partial(terms_kernel, groups, cuts, tile), grid=...  23.1 us
    pallas_call x1, Pallas kernels, apply_rows(): pl.pallas_call(functools.partial(apply_kernel, groups, cuts, tile, denom)...  13.7 us

profile of v1, /device:TPU:19, one launch (start us, length us, event | category | flops | bytes accessed | tf_op | source)
XLA Modules:
  0.0 141.4 jit_solution(15964843387700046715)
XLA Ops:
  0.0 1.2 dynamic_slice.3.count_ref
  1.2 0.6 fusion
  1.8 0.7 multiply_multiply_fusion
  2.5 1.4 copy.20
  3.9 1.6 %fusion.1.own_ref = bf16[2,3,16,512]{3,2,1,0:T(8,128)(2,1)} fusion(f32[2,1,16,512]{3,2,1,0:T(8,128)} %bitcast.35, f32[2,1,16,512]{3,2,1,0:T(8,128)} %bitcast.37, f32[2,1,16,512]{3,2,1,0:T(8,128)} %bitcast.39), kind=kLoop, calls=%fused_computation.4 | loop fusion | flops 98304 | bytes 294912 | tf_op jit(solution)/shard_map/convert_element_type | solution.py:443
  5.4 33.4 %gather_start.1 = bf16[2,3,32,16,512]{4,3,2,1,0:T(8,128)(2,1)} custom-call(bf16[2,3,16,512]{3,2,1,0:T(8,128)(2,1)} %fusion.1.own_ref), custom_call_target="tpu_custom_call" | custom-call | tf_op jit(solution)/shard_map/gather_start/pallas_call | solution.py:170
  38.8 0.0 copy-start
  38.9 0.0 copy-start.1
  38.9 0.0 copy-start.2
  38.9 23.1 %local_terms.1 = bf16[2,3,512,512]{3,2,1,0:T(8,128)(2,1)} custom-call(bf16[16384,128]{1,0:T(8,128)(2,1)} %bitcast.32, bf16[16384,128]{1,0:T(8,128)(2,1)} %bitcast.33, f32[2048,2]{1,0:T(8,128)} %bitcast.34, bf16[2,3,512,512]{3,2,1,0:T(8,128)(2,1)} %bitcast.30), custom_call_target="tpu_custom_call" | custom-call | tf_op jit(solution)/shard_map/local_terms/pallas_call | solution.py:352
  62.0 0.0 copy-done
  62.0 0.0 copy-done.1
  62.0 0.0 copy-done.2
  62.0 0.7 pad_maximum_fusion.w_ref
  62.7 65.0 %reduce_gather.1 = bf16[2,3,32,16,512]{4,3,2,1,0:T(8,128)(2,1)} custom-call(bf16[2,3,16,2,16,512]{5,4,3,2,1,0:T(8,128)(2,1)} %bitcast.29, f32[2,3,16,512]{3,2,1,0:T(8,128)} %pad_maximum_fusion.w_ref), custom_call_target="tpu_custom_call" | custom-call | tf_op jit(solution)/shard_map/reduce_gather/pallas_call | solution.py:265
  127.7 13.7 %apply_rows.1 = bf16[16384,128]{1,0:T(8,128)(2,1)} custom-call(s32[1]{0:T(128)} %dynamic_slice.3.count_ref, f32[2]{0:T(128)} %scale_ref.1, bf16[16384,128]{1,0:T(8,128)(2,1)} %bitcast.31, bf16[2,3,512,512]{3,2,1,0:T(8,128)(2,1)} %bitcast.28), custom_call_target="tpu_custom_call" | custom-call | tf_op jit(solution)/shard_map/apply_rows/pallas_call | solution.py:407
Async XLA Ops:
  38.8 23.2 %copy-start = (f32[2,16,512]{2,1,0:T(8,128)S(1)}, f32[2,16,512]{2,1,0:T(8,128)}, u32[]{:S(2)}) copy-start(f32[2,16,512]{2,1,0:T(8,128)} %param.17) | copy-start | bytes 196612
  38.9 23.2 %copy-start.1 = (f32[2,16,512]{2,1,0:T(8,128)S(1)}, f32[2,16,512]{2,1,0:T(8,128)}, u32[]{:S(2)}) copy-start(f32[2,16,512]{2,1,0:T(8,128)} %param.16) | copy-start | bytes 196612
  38.9 23.2 %copy-start.2 = (f32[2,16,512]{2,1,0:T(8,128)S(1)}, f32[2,16,512]{2,1,0:T(8,128)}, u32[]{:S(2)}) copy-start(f32[2,16,512]{2,1,0:T(8,128)} %param.15) | copy-start | bytes 196612

commit v2 on v1

--- a/solution.py
+++ b/solution.py
@@ -180,7 +180,7 @@
     )(own)
 
 
-def reduce_kernel(n, part_ref, w_ref, out_ref, pair, pair_in, buf_r, buf_l, in_r, in_l, fresh,
+def reduce_kernel(n, part_ref, w_ref, out_ref, pair_in, buf_r, buf_l, in_r, in_l, fresh,
                   xs, xr, rs, rr, ls, lr, *gsems):
     ring = Ring(n)
     groups = w_ref.shape[0]
@@ -268,7 +268,6 @@
         in_specs=[pl.BlockSpec(memory_space=pltpu.VMEM)] * 2,
         out_specs=pl.BlockSpec(memory_space=pltpu.VMEM),
         scratch_shapes=[
-            pltpu.VMEM((8, LANES), bf),
             pltpu.VMEM((groups, kinds, chips, rows, feats), bf),
             pltpu.VMEM((right,) + piece, bf),
             pltpu.VMEM((left,) + piece, bf),
@@ -440,10 +439,11 @@
     full = (groups, 3, feat_width, feat_width)
     chips = seq_size // 2
     own_rows = w_own.shape[2]
-    halves = gather_rows(seq_size, w_own.astype(jnp.bfloat16)).reshape(full)
+    pieces = w_own.reshape(groups * 3, 1, own_rows, feat_width)
+    halves = gather_rows(seq_size, pieces.astype(jnp.bfloat16)).reshape(full)
     part = local_terms(to_view(key_rows), to_view(value_rows), eta_rows, halves)
-    part = part.reshape(groups, 3, chips, 2, own_rows, feat_width)
-    fresh = reduce_rows(seq_size, part, w_own).reshape(full)
+    part = part.reshape(groups * 3, 1, chips, 2, own_rows, feat_width)
+    fresh = reduce_rows(seq_size, part, pieces).reshape(full)
     denom = groups * feat_width * heads
     view = apply_rows(
         to_view(queries), own_count, group_scales, fresh, cap_rows, denom if heads == 1 else None

time: 144 us -> 139 us (0.965)
  Pallas kernels: 135 us -> 131 us
    pallas_call x1, Pallas kernels: 65 us -> 61 us  [reduce_rows(): pl.pallas_call(functools.partial(reduce_kernel, n), out_shape=jax.ShapeDt...]
where the time goes in v2:
time: 139 us; the launch traced here: 137 us
  Pallas kernels  131 us (94%)
  other arithmetic  3.02 us (2%)
  local copies, waits for them, and re-layouts  2.7 us (2%)
    pallas_call x1, Pallas kernels, reduce_rows(): pl.pallas_call(functools.partial(reduce_kernel, n), out_shape=jax.ShapeDt...  61 us
    pallas_call x1, Pallas kernels, gather_rows(): pl.pallas_call(functools.partial(gather_kernel, n), out_shape=jax.ShapeDt...  33 us
    pallas_call x1, Pallas kernels, local_terms(): pl.pallas_call(functools.partial(terms_kernel, groups, cuts, tile), grid=...  23.1 us
    pallas_call x1, Pallas kernels, apply_rows(): pl.pallas_call(functools.partial(apply_kernel, groups, cuts, tile, denom)...  13.8 us

profile of v2, /device:TPU:19, one launch (start us, length us, event | category | flops | bytes accessed | tf_op | source)
XLA Modules:
  0.0 136.7 jit_solution(14828228998578326102)
XLA Ops:
  0.0 1.3 dynamic_slice.3.count_ref
  1.3 0.7 fusion
  2.0 0.7 multiply_multiply_fusion
  2.7 0.9 pad_maximum_fusion
  3.7 0.0 copy-start
  3.7 0.7 convert_element_type.16.own_ref
  4.4 1.4 copy.21
  5.7 33.0 %gather_start.1 = bf16[6,1,32,16,512]{4,3,2,1,0:T(8,128)(2,1)} custom-call(bf16[6,1,16,512]{3,2,1,0:T(8,128)(2,1)} %convert_element_type.16.own_ref), custom_call_target="tpu_custom_call" | custom-call | tf_op jit(solution)/shard_map/gather_start/pallas_call | solution.py:170
  38.7 23.1 %local_terms.1 = bf16[2,3,512,512]{3,2,1,0:T(8,128)(2,1)} custom-call(bf16[16384,128]{1,0:T(8,128)(2,1)} %bitcast.33, bf16[16384,128]{1,0:T(8,128)(2,1)} %bitcast.34, f32[2048,2]{1,0:T(8,128)} %bitcast.35, bf16[2,3,512,512]{3,2,1,0:T(8,128)(2,1)} %bitcast.31), custom_call_target="tpu_custom_call" | custom-call | tf_op jit(solution)/shard_map/local_terms/pallas_call | solution.py:351
  61.9 0.0 copy-done
  61.9 61.0 %reduce_gather.1 = bf16[6,1,32,16,512]{4,3,2,1,0:T(8,128)(2,1)} custom-call(bf16[6,1,16,2,16,512]{5,4,3,2,1,0:T(8,128)(2,1)} %bitcast.30, f32[6,1,16,512]{3,2,1,0:T(8,128)} %bitcast.37), custom_call_target="tpu_custom_call" | custom-call | tf_op jit(solution)/shard_map/reduce_gather/pallas_call | solution.py:265
  122.9 13.8 %apply_rows.1 = bf16[16384,128]{1,0:T(8,128)(2,1)} custom-call(s32[1]{0:T(128)} %dynamic_slice.3.count_ref, f32[2]{0:T(128)} %scale_ref.1, bf16[16384,128]{1,0:T(8,128)(2,1)} %bitcast.32, bf16[2,3,512,512]{3,2,1,0:T(8,128)(2,1)} %bitcast.29), custom_call_target="tpu_custom_call" | custom-call | tf_op jit(solution)/shard_map/apply_rows/pallas_call | solution.py:406
  (1 shorter events, 0.0 us)
Async XLA Ops:
  3.7 58.2 %copy-start = (f32[2,3,16,512]{3,2,1,0:T(8,128)}, f32[2,3,16,512]{3,2,1,0:T(8,128)S(1)}, u32[]{:S(2)}) copy-start(f32[2,3,16,512]{3,2,1,0:T(8,128)S(1)} %copy.22) | copy-start | bytes 589828

commit v3 on v2

v3 whole, which is shorter than its diff:
```python
import functools

import jax
import jax.numpy as jnp
from jax import lax
from jax.experimental import pallas as pl
from jax.experimental.pallas import tpu as pltpu
from jax.sharding import PartitionSpec as P

EPS = 1e-06
MESH = pl.DeviceIdType.MESH
LANES = 128
VMEM_LIMIT = 60 * 1024 * 1024


class Grid:
    def __init__(self, n):
        me = lax.axis_index("seq")
        self.depth = n // 8
        self.core = me % 2
        self.x = (me // 2) % 2
        self.y = (me // 4) % 2
        self.z = me // 8
        self.partner = self.index(self.z, self.y, self.x, 1 - self.core)

    def index(self, z, y, x, core):
        return z * 8 + y * 4 + x * 2 + core

    def place(self, half, near, far):
        flip_y, flip_x = (far, near) if half == 0 else (near, far)
        return (1 - self.y if flip_y else self.y), (1 - self.x if flip_x else self.x)

    def peer(self, half, near, far):
        y, x = self.place(half, near, far)
        return self.index(self.z, y, x, self.core)

    def column(self, step):
        return (self.z + step + self.depth) % self.depth

    def z_peer(self, step):
        return self.index(self.column(step), self.y, self.x, self.core)

    def barrier(self):
        sem = pltpu.get_barrier_semaphore()
        peers = [self.z_peer(k) for k in range(1, self.depth)]
        peers += [self.peer(0, 1, 0), self.peer(0, 0, 1), self.partner]
        for peer in peers:
            pl.semaphore_signal(sem, inc=1, device_id={"seq": peer}, device_id_type=MESH)
        pl.semaphore_wait(sem, len(peers))


def remote(src, dst, send_sem, recv_sem, peer):
    return pltpu.make_async_remote_copy(
        src_ref=src, dst_ref=dst, send_sem=send_sem, recv_sem=recv_sem,
        device_id={"seq": peer}, device_id_type=MESH,
    )


def gather_blocks(grid, own, out, sems):
    zs, zr, ns, nr, fs, fr, ps, pr = sems
    depth = grid.depth
    started = []
    partners = []

    def slot(half, k, near, far):
        y, x = grid.place(half, near, far)
        return out.at[half, :, grid.column(-k), y, x, grid.core]

    def source(half, k, near, far):
        return own.at[half] if (k, near, far) == (0, 0, 0) else slot(half, k, near, far)

    def send(copy):
        copy.start()
        started.append(copy)
        return copy

    def to_near(half, k):
        return remote(source(half, k, 0, 0), slot(half, k, 0, 0),
                      ns.at[half, k], nr.at[half, k], grid.peer(half, 1, 0))

    def to_far(half, k, near):
        return remote(source(half, k, near, 0), slot(half, k, near, 0),
                      fs.at[half, near, k], fr.at[half, near, k], grid.peer(half, 0, 1))

    def to_partner(half, k, near, far):
        copy = remote(source(half, k, near, far), slot(half, k, near, far),
                      ps.at[half, near, far, k], pr.at[half, near, far, k], grid.partner)
        partners.append(send(copy))

    columns = {}
    for k in range(1, depth):
        for half in range(2):
            columns[half, k] = send(remote(own.at[half], slot(half, 0, 0, 0), zs.at[half, k - 1],
                                           zr.at[half, k - 1], grid.z_peer(k)))
    for half in range(2):
        out[half, :, grid.z, grid.y, grid.x, grid.core] = own[half]
    nears, fars = {}, {}
    order = [0] + [k for d in range(1, depth) for k in (d, depth - d) if d <= depth - d]
    order = list(dict.fromkeys(order))
    for i in range(depth + 1):
        for half in range(2):
            if i < depth:
                k = order[i]
                if k > 0:
                    columns[half, k].wait_recv()
                nears[half, k] = send(to_near(half, k))
                fars[half, 0, k] = send(to_far(half, k, 0))
                to_partner(half, k, 0, 0)
            if i > 0:
                k = order[i - 1]
                nears[half, k].wait_recv()
                fars[half, 1, k] = send(to_far(half, k, 1))
                to_partner(half, k, 1, 0)
    for k in order:
        for half in range(2):
            for near in range(2):
                fars[half, near, k].wait_recv()
                to_partner(half, k, near, 1)
    for copy in partners:
        copy.wait_recv()
    for copy in started:
        copy.wait_send()


def gather_sems(n):
    depth = n // 8
    dma = pltpu.SemaphoreType.DMA
    sems = []
    for shape in ((2, max(depth - 1, 1)), (2, depth), (2, 2, depth), (2, 2, 2, depth)):
        sems += [dma(shape), dma(shape)]
    return sems


def gather_kernel(n, own_ref, out_ref, *sems):
    grid = Grid(n)
    grid.barrier()
    gather_blocks(grid, own_ref, out_ref, sems)


def gather_rows(n, own):
    halves, kinds, rows, feats = own.shape
    return pl.pallas_call(
        functools.partial(gather_kernel, n),
        out_shape=jax.ShapeDtypeStruct((halves, kinds, n // 8, 2, 2, 2, rows, feats), own.dtype),
        in_specs=[pl.BlockSpec(memory_space=pltpu.VMEM)],
        out_specs=pl.BlockSpec(memory_space=pltpu.VMEM),
        scratch_shapes=gather_sems(n),
        compiler_params=pltpu.CompilerParams(
            collective_id=0, has_side_effects=True, vmem_limit_bytes=VMEM_LIMIT
        ),
        name="gather_start",
    )(own)


def reduce_kernel(n, part_ref, w_ref, out_ref, pair_in, far_out, far_in, near_out, near_in,
                  z_out, z_in, fresh, xs, xr, fs, fr, ns, nr, zs, zr, *gsems):
    grid = Grid(n)
    depth = grid.depth
    f32 = jnp.float32
    grid.barrier()
    order = list(range(1, depth)) + [0]
    started = []

    def send(copy):
        copy.start()
        started.append(copy)
        return copy

    exchange, fars, nears, columns = {}, {}, {}, {}
    for k in order:
        for half in range(2):
            col = grid.column(k)
            exchange[half, k] = send(remote(
                part_ref.at[half, :, col, :, :, 1 - grid.core], pair_in.at[half, :, k],
                xs.at[half, k], xr.at[half, k], grid.partner))

    def both(half, k, near, far):
        y, x = grid.place(half, near, far)
        return (part_ref[half, :, grid.column(k), y, x, grid.core].astype(f32)
                + pair_in[half, :, k, y, x].astype(f32))

    for k in order:
        for half in range(2):
            exchange[half, k].wait_recv()
            for near in range(2):
                far_out[half, k, near] = both(half, k, near, 1).astype(far_out.dtype)
            fars[half, k] = send(remote(far_out.at[half, k], far_in.at[half, k],
                                        fs.at[half, k], fr.at[half, k], grid.peer(half, 0, 1)))
    for k in order:
        for half in range(2):
            fars[half, k].wait_recv()
            near_out[half, k] = (both(half, k, 1, 0) + far_in[half, k, 1].astype(f32)
                                 ).astype(near_out.dtype)
            nears[half, k] = send(remote(near_out.at[half, k], near_in.at[half, k],
                                         ns.at[half, k], nr.at[half, k], grid.peer(half, 1, 0)))
    totals = [None, None]
    for k in order:
        for half in range(2):
            nears[half, k].wait_recv()
            value = (both(half, k, 0, 0) + far_in[half, k, 0].astype(f32)
                     + near_in[half, k].astype(f32))
            if k == 0:
                totals[half] = value
            else:
                z_out[half, k - 1] = value.astype(z_out.dtype)
                columns[half, k] = send(remote(z_out.at[half, k - 1], z_in.at[half, k - 1],
                                               zs.at[half, k - 1], zr.at[half, k - 1],
                                               grid.z_peer(k)))
    for half in range(2):
        term = totals[half]
        for k in range(1, depth):
            columns[half, k].wait_recv()
            term = term + z_in[half, k - 1].astype(f32)
        start_w = w_ref[half]
        update = start_w + term
        norm_old = jnp.sqrt(jnp.mean(start_w * start_w, axis=-1, keepdims=True) + EPS)
        norm_new = jnp.sqrt(jnp.mean(update * update, axis=-1, keepdims=True) + EPS)
        fresh[half] = (update * (norm_old / norm_new)).astype(fresh.dtype)

    gather_blocks(grid, fresh, out_ref, gsems)
    for copy in started:
        copy.wait_send()


def reduce_rows(n, part, w_own):
    halves, kinds, rows, feats = w_own.shape
    depth = n // 8
    hops = max(depth - 1, 1)
    dma = pltpu.SemaphoreType.DMA
    bf = jnp.bfloat16
    block = (kinds, rows, feats)
    return pl.pallas_call(
        functools.partial(reduce_kernel, n),
        out_shape=jax.ShapeDtypeStruct((halves, kinds, depth, 2, 2, 2, rows, feats), bf),
        in_specs=[pl.BlockSpec(memory_space=pltpu.VMEM)] * 2,
        out_specs=pl.BlockSpec(memory_space=pltpu.VMEM),
        scratch_shapes=[
            pltpu.VMEM((halves, kinds, depth, 2, 2, rows, feats), bf),
            pltpu.VMEM((halves, depth, 2) + block, bf),
            pltpu.VMEM((halves, depth, 2) + block, bf),
            pltpu.VMEM((halves, depth) + block, bf),
            pltpu.VMEM((halves, depth) + block, bf),
            pltpu.VMEM((halves, hops) + block, bf),
            pltpu.VMEM((halves, hops) + block, bf),
            pltpu.VMEM((halves,) + block, bf),
            dma((2, depth)), dma((2, depth)), dma((2, depth)), dma((2, depth)),
            dma((2, depth)), dma((2, depth)), dma((2, hops)), dma((2, hops)),
        ] + gather_sems(n),
        compiler_params=pltpu.CompilerParams(
            collective_id=1, has_side_effects=True, vmem_limit_bytes=VMEM_LIMIT
        ),
        name="reduce_gather",
    )(part, w_own)


def to_view(rows):
    tokens, groups, feats = rows.shape
    cuts = feats // LANES
    return rows.reshape(tokens, groups, cuts, LANES).transpose(0, 2, 1, 3).reshape(-1, LANES)


def from_view(view, shape):
    tokens, groups, feats = shape
    cuts = feats // LANES
    return view.reshape(tokens, cuts, groups, LANES).transpose(0, 2, 1, 3).reshape(shape)


def pick(scr, g, groups, cuts, tile):
    step = groups * cuts
    cols = [scr[pl.ds(c * groups + g, tile, stride=step), :] for c in range(cuts)]
    return jnp.concatenate(cols, axis=-1).astype(jnp.bfloat16)


def dot(a, b, dims):
    return lax.dot_general(a, b, (dims, ((), ())), preferred_element_type=jnp.float32)


def sigmoid(x):
    return 0.5 * jnp.tanh(0.5 * x) + 0.5


def terms_kernel(groups, cuts, tile, k_ref, v_ref, eta_ref, b_ref, out_ref, k_scr, v_scr, acc):
    i = pl.program_id(0)

    @pl.when(i == 0)
    def _():
        acc[...] = jnp.zeros_like(acc)

    k_scr[...] = k_ref[...].astype(jnp.float32)
    v_scr[...] = v_ref[...].astype(jnp.float32)
    for g in range(groups):
        k = pick(k_scr, g, groups, cuts, tile)
        v = pick(v_scr, g, groups, cuts, tile)
        err = (eta_ref[:, g:g + 1] * v.astype(jnp.float32)).astype(jnp.bfloat16)
        h_one = dot(k, b_ref[g, 0], ((1,), (0,)))
        h_three = dot(k, b_ref[g, 1], ((1,), (0,)))
        back = dot(err, b_ref[g, 2], ((1,), (1,)))
        sig = sigmoid(h_one)
        gate = h_one * sig
        act = (gate * h_three).astype(jnp.bfloat16)
        d_one = (back * h_three * (sig * (1.0 + h_one * (1.0 - sig)))).astype(jnp.bfloat16)
        d_three = (back * gate).astype(jnp.bfloat16)
        acc[g, 0] += dot(k, d_one, ((0,), (0,)))
        acc[g, 1] += dot(k, d_three, ((0,), (0,)))
        acc[g, 2] += dot(act, err, ((0,), (0,)))

    @pl.when(i == pl.num_programs(0) - 1)
    def _():
        out_ref[...] = acc[...].astype(out_ref.dtype)


def local_terms(k_view, v_view, eta_rows, halves):
    groups, kinds, width, feats = halves.shape
    cuts = feats // LANES
    tokens = eta_rows.shape[0]
    tile = min(512, tokens)
    rows = tile * groups * cuts
    whole = pl.BlockSpec(memory_space=pltpu.VMEM)
    return pl.pallas_call(
        functools.partial(terms_kernel, groups, cuts, tile),
        grid=(tokens // tile,),
        out_shape=jax.ShapeDtypeStruct(halves.shape, jnp.bfloat16),
        in_specs=[
            pl.BlockSpec((rows, LANES), lambda i: (i, 0)),
            pl.BlockSpec((rows, LANES), lambda i: (i, 0)),
            pl.BlockSpec((tile, groups), lambda i: (i, 0)),
            whole,
        ],
        out_specs=whole,
        scratch_shapes=[
            pltpu.VMEM((rows, LANES), jnp.float32),
            pltpu.VMEM((rows, LANES), jnp.float32),
            pltpu.VMEM(halves.shape, jnp.float32),
        ],
        compiler_params=pltpu.CompilerParams(vmem_limit_bytes=VMEM_LIMIT),
        name="local_terms",
    )(k_view, v_view, eta_rows, halves)


def apply_kernel(groups, cuts, tile, denom, count_ref, scale_ref, q_ref, c_ref, out_ref, q_scr, o_scr):
    i = pl.program_id(0)
    step = groups * cuts
    position = i * tile + lax.broadcasted_iota(jnp.int32, (tile, 1), 0)
    live = (position < count_ref[0]).astype(jnp.float32)
    q_scr[...] = q_ref[...].astype(jnp.float32)
    pieces = []
    total_sq = jnp.zeros((tile, 1), jnp.float32)
    for g in range(groups):
        q = pick(q_scr, g, groups, cuts, tile)
        q_one = dot(q, c_ref[g, 0], ((1,), (0,)))
        q_three = dot(q, c_ref[g, 1], ((1,), (0,)))
        a_query = (q_one * sigmoid(q_one) * q_three).astype(jnp.bfloat16)
        o = dot(a_query, c_ref[g, 2], ((1,), (0,))).astype(jnp.bfloat16)
        o = o.astype(jnp.float32) * live
        if denom is not None:
            o = o * scale_ref[g]
            total_sq = total_sq + jnp.sum(o * o, axis=-1, keepdims=True)
        pieces.append(o)
    if denom is not None:
        factor = lax.rsqrt(total_sq / denom + EPS)
        pieces = [o * factor for o in pieces]
    for g in range(groups):
        for c in range(cuts):
            o_scr[pl.ds(c * groups + g, tile, stride=step), :] = pieces[g][:, c * LANES:(c + 1) * LANES]
    out_ref[...] = o_scr[...].astype(out_ref.dtype)


def apply_rows(q_view, count, scales, fresh, tokens, denom):
    groups, kinds, width, feats = fresh.shape
    cuts = feats // LANES
    tile = min(512, tokens)
    rows = tile * groups * cuts
    smem = pl.BlockSpec(memory_space=pltpu.SMEM)
    return pl.pallas_call(
        functools.partial(apply_kernel, groups, cuts, tile, denom),
        grid=(tokens // tile,),
        out_shape=jax.ShapeDtypeStruct(q_view.shape, jnp.bfloat16),
        in_specs=[
            smem,
            smem,
            pl.BlockSpec((rows, LANES), lambda i: (i, 0)),
            pl.BlockSpec(memory_space=pltpu.VMEM),
        ],
        out_specs=pl.BlockSpec((rows, LANES), lambda i: (i, 0)),
        scratch_shapes=[
            pltpu.VMEM((rows, LANES), jnp.float32),
            pltpu.VMEM((rows, LANES), jnp.float32),
        ],
        compiler_params=pltpu.CompilerParams(vmem_limit_bytes=VMEM_LIMIT),
        name="apply_rows",
    )(count, scales, q_view, fresh)


def shards(
    queries, key_rows, value_rows, step_rates, live_counts, group_scales, w_first, w_third, w_second
):
    cap_rows, groups, feat_width = queries.shape
    seq_size = lax.axis_size("seq")
    heads = lax.axis_size("heads")
    root_total = jnp.sqrt(jnp.float32(cap_rows * seq_size))
    own_count = lax.dynamic_slice(live_counts, (lax.axis_index("seq"),), (1,))
    live_mask = jnp.arange(cap_rows, dtype=jnp.int32) < own_count[0]
    eta_rows = (
        step_rates.T.astype(jnp.float32) * live_mask.astype(jnp.float32)[:, None] / root_total
    )
    w_own = jnp.stack([w_first, w_third, w_second], axis=1)
    full = (groups, 3, feat_width, feat_width)
    own_rows = w_own.shape[2]
    pieces = w_own.reshape(2, groups * 3 // 2, own_rows, feat_width)
    halves = gather_rows(seq_size, pieces.astype(jnp.bfloat16)).reshape(full)
    part = local_terms(to_view(key_rows), to_view(value_rows), eta_rows, halves)
    part = part.reshape(2, groups * 3 // 2, seq_size // 8, 2, 2, 2, own_rows, feat_width)
    fresh = reduce_rows(seq_size, part, pieces).reshape(full)
    denom = groups * feat_width * heads
    view = apply_rows(
        to_view(queries), own_count, group_scales, fresh, cap_rows, denom if heads == 1 else None
    )
    fast = from_view(view, queries.shape)
    if heads == 1:
        return fast
    wide = fast.astype(jnp.float32) * group_scales[None, :, None]
    total_sq = lax.psum(jnp.sum(wide * wide, axis=(1, 2)), "heads")
    factor = lax.rsqrt(total_sq / denom + EPS)[:, None, None]
    return (wide * factor).astype(jnp.bfloat16)


def solution(mesh):
    in_specs = (
        P("seq", "heads", None),
        P("seq", "heads", None),
        P("seq", "heads", None),
        P("heads", "seq"),
        P(),
        P("heads"),
        P("heads", "seq", None),
        P("heads", "seq", None),
        P("heads", "seq", None),
    )
    out_specs = P("seq", "heads", None)
    return jax.shard_map(shards, mesh=mesh, in_specs=in_specs, out_specs=out_specs, check_vma=False)
```

time: 139 us -> 125 us (0.90); the launches traced: 137 us -> 124 us
  Pallas kernels: 131 us -> 118 us
    pallas_call x1, Pallas kernels: 61 us -> 53.5 us  [reduce_rows(): pl.pallas_call(functools.partial(reduce_kernel, n), out_shape=jax.ShapeDt...]
    pallas_call x1, Pallas kernels: 33 us -> 27.8 us  [gather_rows(): pl.pallas_call(functools.partial(gather_kernel, n), out_shape=jax.ShapeDt...]
where the time goes in v3:
time: 125 us; the launch traced here: 124 us
  Pallas kernels  118 us (94%)
  other arithmetic  3.53 us (3%)
  local copies, waits for them, and re-layouts  2.6 us (2%)
    pallas_call x1, Pallas kernels, reduce_rows(): pl.pallas_call(functools.partial(reduce_kernel, n), out_shape=jax.ShapeDt...  53.5 us
    pallas_call x1, Pallas kernels, gather_rows(): pl.pallas_call(functools.partial(gather_kernel, n), out_shape=jax.ShapeDt...  27.8 us
    pallas_call x1, Pallas kernels, local_terms(): pl.pallas_call(functools.partial(terms_kernel, groups, cuts, tile), grid=...  23.1 us
    pallas_call x1, Pallas kernels, apply_rows(): pl.pallas_call(functools.partial(apply_kernel, groups, cuts, tile, denom)...  13.7 us

profile of v3, /device:TPU:19, one launch (start us, length us, event | category | flops | bytes accessed | tf_op | source)
XLA Modules:
  0.0 124.3 jit_solution(553479980788062550)
XLA Ops:
  0.0 1.2 dynamic_slice.3.count_ref
  1.2 0.6 fusion
  1.8 0.7 multiply_multiply_fusion
  2.5 1.4 %copy.20 = f32[2,2048]{0,1:T(8,128)} copy(f32[2,2048]{1,0:T(2,128)S(1)} %multiply_multiply_fusion) | data formatting | bytes 32768 | tf_op jit(solution)/shard_map/div | solution.py:404
  3.9 1.6 %fusion.1.own_ref = bf16[2,3,16,512]{3,2,1,0:T(8,128)(2,1)} fusion(f32[2,1,16,512]{3,2,1,0:T(8,128)} %bitcast.35, f32[2,1,16,512]{3,2,1,0:T(8,128)} %bitcast.37, f32[2,1,16,512]{3,2,1,0:T(8,128)} %bitcast.39), kind=kLoop, calls=%fused_computation.4 | loop fusion | flops 98304 | bytes 294912 | tf_op jit(solution)/shard_map/convert_element_type | solution.py:410
  5.4 27.8 %gather_start.1 = bf16[2,3,4,2,2,2,16,512]{7,6,5,4,3,2,1,0:T(8,128)(2,1)} custom-call(bf16[2,3,16,512]{3,2,1,0:T(8,128)(2,1)} %fusion.1.own_ref), custom_call_target="tpu_custom_call" | custom-call | tf_op jit(solution)/shard_map/gather_start/pallas_call | solution.py:142
  33.2 0.0 copy-start
  33.3 0.0 copy-start.1
  33.3 0.0 copy-start.2
  33.3 23.1 %local_terms.1 = bf16[2,3,512,512]{3,2,1,0:T(8,128)(2,1)} custom-call(bf16[16384,128]{1,0:T(8,128)(2,1)} %bitcast.32, bf16[16384,128]{1,0:T(8,128)(2,1)} %bitcast.33, f32[2048,2]{1,0:T(8,128)} %bitcast.34, bf16[2,3,512,512]{3,2,1,0:T(8,128)(2,1)} %bitcast.30), custom_call_target="tpu_custom_call" | custom-call | tf_op jit(solution)/shard_map/local_terms/pallas_call | solution.py:319
  56.4 0.0 copy-done
  56.4 0.0 copy-done.1
  56.4 0.0 copy-done.2
  56.4 0.7 pad_maximum_fusion.w_ref
  57.1 53.5 %reduce_gather.1 = bf16[2,3,4,2,2,2,16,512]{7,6,5,4,3,2,1,0:T(8,128)(2,1)} custom-call(bf16[2,3,4,2,2,2,16,512]{7,6,5,4,3,2,1,0:T(8,128)(2,1)} %bitcast.29, f32[2,3,16,512]{3,2,1,0:T(8,128)} %pad_maximum_fusion.w_ref), custom_call_target="tpu_custom_call" | custom-call | tf_op jit(solution)/shard_map/reduce_gather/pallas_call | solution.py:232
  110.6 13.7 %apply_rows.1 = bf16[16384,128]{1,0:T(8,128)(2,1)} custom-call(s32[1]{0:T(128)} %dynamic_slice.3.count_ref, f32[2]{0:T(128)} %scale_ref.1, bf16[16384,128]{1,0:T(8,128)(2,1)} %bitcast.31, bf16[2,3,512,512]{3,2,1,0:T(8,128)(2,1)} %bitcast.28), custom_call_target="tpu_custom_call" | custom-call | tf_op jit(solution)/shard_map/apply_rows/pallas_call | solution.py:374
Async XLA Ops:
  33.2 23.2 %copy-start = (f32[2,16,512]{2,1,0:T(8,128)S(1)}, f32[2,16,512]{2,1,0:T(8,128)}, u32[]{:S(2)}) copy-start(f32[2,16,512]{2,1,0:T(8,128)} %param.17) | copy-start | bytes 196612
  33.3 23.2 %copy-start.1 = (f32[2,16,512]{2,1,0:T(8,128)S(1)}, f32[2,16,512]{2,1,0:T(8,128)}, u32[]{:S(2)}) copy-start(f32[2,16,512]{2,1,0:T(8,128)} %param.16) | copy-start | bytes 196612
  33.3 23.2 %copy-start.2 = (f32[2,16,512]{2,1,0:T(8,128)S(1)}, f32[2,16,512]{2,1,0:T(8,128)}, u32[]{:S(2)}) copy-start(f32[2,16,512]{2,1,0:T(8,128)} %param.15) | copy-start | bytes 196612

commit v4 on v3

--- a/solution.py
+++ b/solution.py
@@ -1,4 +1,5 @@
 import functools
+import math
 
 import jax
 import jax.numpy as jnp
@@ -279,19 +280,24 @@
     return 0.5 * jnp.tanh(0.5 * x) + 0.5
 
 
-def terms_kernel(groups, cuts, tile, k_ref, v_ref, eta_ref, b_ref, out_ref, k_scr, v_scr, acc):
+def terms_kernel(groups, cuts, tile, root, count_ref, k_ref, v_ref, rate_ref, b_ref, out_ref, k_scr, v_scr, acc):
     i = pl.program_id(0)
 
     @pl.when(i == 0)
     def _():
         acc[...] = jnp.zeros_like(acc)
 
+    position = i * tile + lax.broadcasted_iota(jnp.int32, (tile, 1), 0)
+    live = (position < count_ref[lax.axis_index("seq")]).astype(jnp.float32)
+    rates = rate_ref[...].astype(jnp.float32)
     k_scr[...] = k_ref[...].astype(jnp.float32)
     v_scr[...] = v_ref[...].astype(jnp.float32)
     for g in range(groups):
         k = pick(k_scr, g, groups, cuts, tile)
         v = pick(v_scr, g, groups, cuts, tile)
-        err = (eta_ref[:, g:g + 1] * v.astype(jnp.float32)).astype(jnp.bfloat16)
+        column = jnp.broadcast_to(rates[g:g + 1], (8, tile)).T[:, 0:1]
+        eta = column * live / root
+        err = (eta * v.astype(jnp.float32)).astype(jnp.bfloat16)
         h_one = dot(k, b_ref[g, 0], ((1,), (0,)))
         h_three = dot(k, b_ref[g, 1], ((1,), (0,)))
         back = dot(err, b_ref[g, 2], ((1,), (1,)))
@@ -309,21 +315,22 @@
         out_ref[...] = acc[...].astype(out_ref.dtype)
 
 
-def local_terms(k_view, v_view, eta_rows, halves):
+def local_terms(k_view, v_view, rates, counts, halves, root):
     groups, kinds, width, feats = halves.shape
     cuts = feats // LANES
-    tokens = eta_rows.shape[0]
+    tokens = rates.shape[1]
     tile = min(512, tokens)
     rows = tile * groups * cuts
     whole = pl.BlockSpec(memory_space=pltpu.VMEM)
     return pl.pallas_call(
-        functools.partial(terms_kernel, groups, cuts, tile),
+        functools.partial(terms_kernel, groups, cuts, tile, root),
         grid=(tokens // tile,),
         out_shape=jax.ShapeDtypeStruct(halves.shape, jnp.bfloat16),
         in_specs=[
+            pl.BlockSpec(memory_space=pltpu.SMEM),
             pl.BlockSpec((rows, LANES), lambda i: (i, 0)),
             pl.BlockSpec((rows, LANES), lambda i: (i, 0)),
-            pl.BlockSpec((tile, groups), lambda i: (i, 0)),
+            pl.BlockSpec((groups, tile), lambda i: (0, i)),
             whole,
         ],
         out_specs=whole,
@@ -334,14 +341,14 @@
         ],
         compiler_params=pltpu.CompilerParams(vmem_limit_bytes=VMEM_LIMIT),
         name="local_terms",
-    )(k_view, v_view, eta_rows, halves)
+    )(counts, k_view, v_view, rates, halves)
 
 
 def apply_kernel(groups, cuts, tile, denom, count_ref, scale_ref, q_ref, c_ref, out_ref, q_scr, o_scr):
     i = pl.program_id(0)
     step = groups * cuts
     position = i * tile + lax.broadcasted_iota(jnp.int32, (tile, 1), 0)
-    live = (position < count_ref[0]).astype(jnp.float32)
+    live = (position < count_ref[lax.axis_index("seq")]).astype(jnp.float32)
     q_scr[...] = q_ref[...].astype(jnp.float32)
     pieces = []
     total_sq = jnp.zeros((tile, 1), jnp.float32)
@@ -397,23 +404,20 @@
     cap_rows, groups, feat_width = queries.shape
     seq_size = lax.axis_size("seq")
     heads = lax.axis_size("heads")
-    root_total = jnp.sqrt(jnp.float32(cap_rows * seq_size))
-    own_count = lax.dynamic_slice(live_counts, (lax.axis_index("seq"),), (1,))
-    live_mask = jnp.arange(cap_rows, dtype=jnp.int32) < own_count[0]
-    eta_rows = (
-        step_rates.T.astype(jnp.float32) * live_mask.astype(jnp.float32)[:, None] / root_total
-    )
+    root_total = math.sqrt(cap_rows * seq_size)
     w_own = jnp.stack([w_first, w_third, w_second], axis=1)
     full = (groups, 3, feat_width, feat_width)
     own_rows = w_own.shape[2]
     pieces = w_own.reshape(2, groups * 3 // 2, own_rows, feat_width)
     halves = gather_rows(seq_size, pieces.astype(jnp.bfloat16)).reshape(full)
-    part = local_terms(to_view(key_rows), to_view(value_rows), eta_rows, halves)
+    part = local_terms(
+        to_view(key_rows), to_view(value_rows), step_rates, live_counts, halves, root_total
+    )
     part = part.reshape(2, groups * 3 // 2, seq_size // 8, 2, 2, 2, own_rows, feat_width)
     fresh = reduce_rows(seq_size, part, pieces).reshape(full)
     denom = groups * feat_width * heads
     view = apply_rows(
-        to_view(queries), own_count, group_scales, fresh, cap_rows, denom if heads == 1 else None
+        to_view(queries), live_counts, group_scales, fresh, cap_rows, denom if heads == 1 else None
     )
     fast = from_view(view, queries.shape)
     if heads == 1:

time: 125 us -> 121 us (0.968)
  local copies, waits for them, and re-layouts: 2.6 us -> 0 us
    div x1 -> x0, local copies, waits for them, and re-layouts: 1.35 us -> none  [shards(): step_rates.T.astype(jnp.float32) * live_mask.astype(jnp.float32)[:, None]]
where the time goes in v4:
time: 121 us
  Pallas kernels  117 us (97%)
  other arithmetic  3.15 us (3%)
    pallas_call x1, Pallas kernels, reduce_rows(): pl.pallas_call(functools.partial(reduce_kernel, n), out_shape=jax.ShapeDt...  53.5 us
    pallas_call x1, Pallas kernels, gather_rows(): pl.pallas_call(functools.partial(gather_kernel, n), out_shape=jax.ShapeDt...  27.8 us
    pallas_call x1, Pallas kernels, local_terms(): pl.pallas_call(functools.partial(terms_kernel, groups, cuts, tile, root),...  22.9 us
    pallas_call x1, Pallas kernels, apply_rows(): pl.pallas_call(functools.partial(apply_kernel, groups, cuts, tile, denom)...  13.2 us

profile of v4, /device:TPU:19, one launch (start us, length us, event | category | flops | bytes accessed | tf_op | source)
XLA Modules:
  0.0 120.6 jit_solution(2689064419301263365)
XLA Ops:
  0.0 1.6 %fusion.own_ref = bf16[2,3,16,512]{3,2,1,0:T(8,128)(2,1)} fusion(f32[2,1,16,512]{3,2,1,0:T(8,128)} %bitcast.32, f32[2,1,16,512]{3,2,1,0:T(8,128)} %bitcast.34, f32[2,1,16,512]{3,2,1,0:T(8,128)} %bitcast.36), kind=kLoop, calls=%fused_computation.1 | loop fusion | flops 98304 | bytes 294912 | tf_op jit(solution)/shard_map/convert_element_type | solution.py:412
  1.6 1.6 %pad_maximum_fusion.w_ref = f32[2,3,16,512]{3,2,1,0:T(8,128)} fusion(f32[2,1,16,512]{3,2,1,0:T(8,128)} %bitcast.33, f32[2,1,16,512]{3,2,1,0:T(8,128)} %bitcast.35, f32[2,1,16,512]{3,2,1,0:T(8,128)} %bitcast.37), kind=kLoop, calls=%fused_computation | loop fusion | flops 98304 | bytes 393216 | tf_op jit(solution)/shard_map/stack | solution.py:408
  3.2 27.8 %gather_start.1 = bf16[2,3,4,2,2,2,16,512]{7,6,5,4,3,2,1,0:T(8,128)(2,1)} custom-call(bf16[2,3,16,512]{3,2,1,0:T(8,128)(2,1)} %fusion.own_ref), custom_call_target="tpu_custom_call" | custom-call | tf_op jit(solution)/shard_map/gather_start/pallas_call | solution.py:143
  31.0 22.9 %local_terms.1 = bf16[2,3,512,512]{3,2,1,0:T(8,128)(2,1)} custom-call(s32[32]{0:T(128)} %count_ref.3, bf16[16384,128]{1,0:T(8,128)(2,1)} %bitcast.30, bf16[16384,128]{1,0:T(8,128)(2,1)} %bitcast.31, bf16[2,2048]{1,0:T(2,128)(2,1)} %rate_ref.1, bf16[2,3,512,512]{3,2,1,0:T(8,128)(2,1)} %bitcast.28), custom_call_target="tpu_custom_call" | custom-call | tf_op jit(solution)/shard_map/local_terms/pallas_call | solution.py:325
  53.9 53.5 %reduce_gather.1 = bf16[2,3,4,2,2,2,16,512]{7,6,5,4,3,2,1,0:T(8,128)(2,1)} custom-call(bf16[2,3,4,2,2,2,16,512]{7,6,5,4,3,2,1,0:T(8,128)(2,1)} %bitcast.27, f32[2,3,16,512]{3,2,1,0:T(8,128)} %pad_maximum_fusion.w_ref), custom_call_target="tpu_custom_call" | custom-call | tf_op jit(solution)/shard_map/reduce_gather/pallas_call | solution.py:233
  107.4 13.2 %apply_rows.1 = bf16[16384,128]{1,0:T(8,128)(2,1)} custom-call(s32[32]{0:T(128)} %count_ref.3, f32[2]{0:T(128)} %scale_ref.1, bf16[16384,128]{1,0:T(8,128)(2,1)} %bitcast.29, bf16[2,3,512,512]{3,2,1,0:T(8,128)(2,1)} %bitcast.26), custom_call_target="tpu_custom_call" | custom-call | tf_op jit(solution)/shard_map/apply_rows/pallas_call | solution.py:381

commit v5 on v4

--- a/solution.py
+++ b/solution.py
@@ -180,22 +180,25 @@
         return (part_ref[half, :, grid.column(k), y, x, grid.core].astype(f32)
                 + pair_in[half, :, k, y, x].astype(f32))
 
-    for k in order:
+    def far_stage(k):
         for half in range(2):
             exchange[half, k].wait_recv()
             for near in range(2):
                 far_out[half, k, near] = both(half, k, near, 1).astype(far_out.dtype)
             fars[half, k] = send(remote(far_out.at[half, k], far_in.at[half, k],
                                         fs.at[half, k], fr.at[half, k], grid.peer(half, 0, 1)))
-    for k in order:
+
+    def near_stage(k):
         for half in range(2):
             fars[half, k].wait_recv()
             near_out[half, k] = (both(half, k, 1, 0) + far_in[half, k, 1].astype(f32)
                                  ).astype(near_out.dtype)
             nears[half, k] = send(remote(near_out.at[half, k], near_in.at[half, k],
                                          ns.at[half, k], nr.at[half, k], grid.peer(half, 1, 0)))
+
     totals = [None, None]
-    for k in order:
+
+    def column_stage(k):
         for half in range(2):
             nears[half, k].wait_recv()
             value = (both(half, k, 0, 0) + far_in[half, k, 0].astype(f32)
@@ -207,6 +210,14 @@
                 columns[half, k] = send(remote(z_out.at[half, k - 1], z_in.at[half, k - 1],
                                                zs.at[half, k - 1], zr.at[half, k - 1],
                                                grid.z_peer(k)))
+
+    for i in range(depth + 2):
+        if i < depth:
+            far_stage(order[i])
+        if 0 < i <= depth:
+            near_stage(order[i - 1])
+        if i > 1:
+            column_stage(order[i - 2])
     for half in range(2):
         term = totals[half]
         for k in range(1, depth):

time: 121 us -> 116 us (0.959)
  Pallas kernels: 117 us -> 112 us
    pallas_call x1, Pallas kernels: 53.5 us -> 48.5 us  [reduce_rows(): pl.pallas_call(functools.partial(reduce_kernel, n), out_shape=jax.ShapeDt...]
where the time goes in v5:
time: 116 us
  Pallas kernels  112 us (97%)
  other arithmetic  3.15 us (3%)
    pallas_call x1, Pallas kernels, reduce_rows(): pl.pallas_call(functools.partial(reduce_kernel, n), out_shape=jax.ShapeDt...  48.5 us
    pallas_call x1, Pallas kernels, gather_rows(): pl.pallas_call(functools.partial(gather_kernel, n), out_shape=jax.ShapeDt...  27.8 us
    pallas_call x1, Pallas kernels, local_terms(): pl.pallas_call(functools.partial(terms_kernel, groups, cuts, tile, root),...  22.9 us
    pallas_call x1, Pallas kernels, apply_rows(): pl.pallas_call(functools.partial(apply_kernel, groups, cuts, tile, denom)...  13.2 us

profile of v5, /device:TPU:19, one launch (start us, length us, event | category | flops | bytes accessed | tf_op | source)
XLA Modules:
  0.0 115.6 jit_solution(3156235027611285429)
XLA Ops:
  0.0 1.6 %fusion.own_ref = bf16[2,3,16,512]{3,2,1,0:T(8,128)(2,1)} fusion(f32[2,1,16,512]{3,2,1,0:T(8,128)} %bitcast.32, f32[2,1,16,512]{3,2,1,0:T(8,128)} %bitcast.34, f32[2,1,16,512]{3,2,1,0:T(8,128)} %bitcast.36), kind=kLoop, calls=%fused_computation.1 | loop fusion | flops 98304 | bytes 294912 | tf_op jit(solution)/shard_map/convert_element_type | solution.py:423
  1.6 1.6 %pad_maximum_fusion.w_ref = f32[2,3,16,512]{3,2,1,0:T(8,128)} fusion(f32[2,1,16,512]{3,2,1,0:T(8,128)} %bitcast.33, f32[2,1,16,512]{3,2,1,0:T(8,128)} %bitcast.35, f32[2,1,16,512]{3,2,1,0:T(8,128)} %bitcast.37), kind=kLoop, calls=%fused_computation | loop fusion | flops 98304 | bytes 393216 | tf_op jit(solution)/shard_map/stack | solution.py:419
  3.2 27.8 %gather_start.1 = bf16[2,3,4,2,2,2,16,512]{7,6,5,4,3,2,1,0:T(8,128)(2,1)} custom-call(bf16[2,3,16,512]{3,2,1,0:T(8,128)(2,1)} %fusion.own_ref), custom_call_target="tpu_custom_call" | custom-call | tf_op jit(solution)/shard_map/gather_start/pallas_call | solution.py:143
  31.0 22.9 %local_terms.1 = bf16[2,3,512,512]{3,2,1,0:T(8,128)(2,1)} custom-call(s32[32]{0:T(128)} %count_ref.3, bf16[16384,128]{1,0:T(8,128)(2,1)} %bitcast.30, bf16[16384,128]{1,0:T(8,128)(2,1)} %bitcast.31, bf16[2,2048]{1,0:T(2,128)(2,1)} %rate_ref.1, bf16[2,3,512,512]{3,2,1,0:T(8,128)(2,1)} %bitcast.28), custom_call_target="tpu_custom_call" | custom-call | tf_op jit(solution)/shard_map/local_terms/pallas_call | solution.py:336
  53.9 48.5 %reduce_gather.1 = bf16[2,3,4,2,2,2,16,512]{7,6,5,4,3,2,1,0:T(8,128)(2,1)} custom-call(bf16[2,3,4,2,2,2,16,512]{7,6,5,4,3,2,1,0:T(8,128)(2,1)} %bitcast.27, f32[2,3,16,512]{3,2,1,0:T(8,128)} %pad_maximum_fusion.w_ref), custom_call_target="tpu_custom_call" | custom-call | tf_op jit(solution)/shard_map/reduce_gather/pallas_call | solution.py:244
  102.4 13.2 %apply_rows.1 = bf16[16384,128]{1,0:T(8,128)(2,1)} custom-call(s32[32]{0:T(128)} %count_ref.3, f32[2]{0:T(128)} %scale_ref.1, bf16[16384,128]{1,0:T(8,128)(2,1)} %bitcast.29, bf16[2,3,512,512]{3,2,1,0:T(8,128)(2,1)} %bitcast.26), custom_call_target="tpu_custom_call" | custom-call | tf_op jit(solution)/shard_map/apply_rows/pallas_call | solution.py:392
